TPU v7x, 128 devices: a whole 4x4x4 slice. The times are simulated.
128 devices in a mesh: row: 8 (over y, core), col: 16 (over x, z).
Axes of the slice: x: 4, y: 4, z: 4, core: 2. Of those that a mesh axis runs over, the one named last changes fastest.
Arguments:
- points: bfloat16 [262144, 512], P(('row', 'col')), may hold values from -6 to 6
- targets: float32 [262144, 256], P(('row', 'col'))
- plan: int32 [6], replicated, may hold values from 0 to 511
- block_inverse: float32 [6, 512, 512], replicated
Outputs:
- residual: float32 [262144, 256], P(('row', 'col'))
- block_steps: bfloat16 [6, 512, 256], replicated
- losses: float32 [6], replicated
All inputs are finite; a program needn't handle non-finite values.
Results may differ from a plain program's by a relative error of at most 0.0062.
Values may be sent and summed in bfloat16 or wider, within the bound.
A program may use at most 64 MiB of HBM per device.

v0:
```python
import jax
import jax.numpy as jnp
from jax import lax
from jax.sharding import PartitionSpec as P

RIDGE = 1.0


def broadcast(block, axis, owner):
    block = jnp.where(lax.axis_index(axis) == owner, block, jnp.zeros_like(block))
    return lax.psum(block, axis)


def route(payload, owner):
    return (
        broadcast(payload[0], ("row", "col"), owner),
        broadcast(payload[1], ("row", "col"), owner),
    )


def on_device(points, targets, plan, block_inverse):
    rows, features = points.shape
    width = targets.shape[1]
    blocksize = block_inverse.shape[1]
    rounds = block_inverse.shape[0]
    across = lax.axis_size("col")
    devices = lax.axis_size("row") * across
    here = lax.axis_index("row") * across + lax.axis_index("col")
    gamma = 2.0 / features
    total = rows * devices * width
    sqnorm = jnp.sum(jnp.square(points.astype(jnp.float32)), axis=1)
    residual = targets
    owners = []
    offsets = []
    for r in range(rounds):
        start = plan[r] * blocksize
        owner = start // rows
        owners.append(owner)
        offsets.append(jnp.clip(start - here * rows, 0, rows - blocksize))
    losses = []
    updates = []
    for r in range(rounds):
        owner = owners[r]
        offset = offsets[r]
        mine = owner == here
        local_rows = lax.dynamic_slice_in_dim(residual, offset, blocksize, 0)
        step = jnp.dot(block_inverse[r], local_rows, precision=lax.Precision.HIGHEST)
        step_half = step.astype(jnp.bfloat16)
        local_points = lax.dynamic_slice_in_dim(points, offset, blocksize, 0)
        block_points, shared_step = route((local_points, step_half), owner)
        updates.append(shared_step)
        block_norm = jnp.sum(jnp.square(block_points.astype(jnp.float32)), axis=1)
        inner = lax.dot_general(
            points, block_points, (((1,), (1,)), ((), ())), preferred_element_type=jnp.float32
        )
        kernel = jnp.exp(-gamma * (sqnorm[:, None] + block_norm[None, :] - 2.0 * inner)).astype(
            jnp.bfloat16
        )
        residual = residual - jnp.dot(kernel, shared_step, preferred_element_type=jnp.float32)
        owned = lax.dynamic_slice_in_dim(residual, offset, blocksize, 0)
        owned = jnp.where(mine, owned - RIDGE * step, owned)
        residual = lax.dynamic_update_slice_in_dim(residual, owned, offset, 0)
        partial_sum = jnp.sum(residual * residual)
        losses.append(lax.psum(partial_sum, ("row", "col")) / total)
    result = jnp.stack(losses)
    return (residual, jnp.stack(updates), result)


def solution(mesh):
    placed = (P(("row", "col"), None), P(("row", "col"), None), P(), P())
    return jax.shard_map(
        on_device,
        mesh=mesh,
        in_specs=placed,
        out_specs=(P(("row", "col"), None), P(), P()),
        check_vma=False,
    )
```

profile of v0, /device:TPU:1, one launch (start us, length us, event | category | flops | bytes accessed | tf_op | source)
XLA Modules:
  0.0 1069.5 jit_solution(4974301191223190520)
XLA Ops:
  7.2 0.0 all-reduce.24.cloned.1.call-start
  7.2 1.5 fusion.54
  12.8 4.0 convert_select_fusion.5
  16.8 2.2 dynamic-slice_select_fusion
  19.0 0.0 all-reduce.24.cloned.1.call-update
  19.0 0.0 all-reduce.22.cloned.1.call-start
  19.1 2.9 copy.7
  22.0 0.5 multiply_reduce_fusion
  22.5 147.7 %all-reduce.24.cloned.1.call-done = (bf16[512,256]{0,1:T(8,128)(2,1)}, bf16[512,512]{1,0:T(8,128)(2,1)}) async-done(((bf16[512,256]{0,1:T(8,128)(2,1)}, bf16[512,512]{1,0:T(8,128)(2,1)}), (bf16[512,256]{0,1:T(8,128)(2,1)}, bf16[512,512]{1,0:T(8,128)(2,1)})) %all-reduce.24.cloned.1.call-update) | async-done | bytes 786448 | tf_op jit(solution)/shard_map/psum | solution.py:11
  170.2 1.2 multiply_reduce_fusion.12
  171.4 5.4 convolution_subtract_fusion.5
  176.8 1.2 subtract_select_fusion.5
  178.0 2.8 dynamic_update_slice.18
  180.9 3.2 convert_select_fusion.4
  184.1 0.0 all-reduce.22.cloned.1.call-update
  184.2 0.2 all-reduce.20.cloned.1.call-start
  184.4 2.7 multiply_reduce_fusion.6
  187.1 0.7 bitcast_dynamic-update-slice_fusion.5
  187.8 143.4 %all-reduce.22.cloned.1.call-done = (bf16[512,256]{0,1:T(8,128)(2,1)}, bf16[512,512]{1,0:T(8,128)(2,1)}) async-done(((bf16[512,256]{0,1:T(8,128)(2,1)}, bf16[512,512]{1,0:T(8,128)(2,1)}), (bf16[512,256]{0,1:T(8,128)(2,1)}, bf16[512,512]{1,0:T(8,128)(2,1)})) %all-reduce.22.cloned.1.call-update) | async-done | bytes 786448 | tf_op jit(solution)/shard_map/psum | solution.py:11
  331.2 1.2 multiply_reduce_fusion.11
  332.4 5.4 convolution_subtract_fusion.4
  337.8 1.3 subtract_select_fusion.4
  339.1 3.5 dynamic_update_slice.19
  342.6 3.3 convert_select_fusion.3
  345.9 0.0 all-reduce.18.cloned.1.call-start
  345.9 2.7 multiply_reduce_fusion.5
  348.7 0.7 bitcast_dynamic-update-slice_fusion.4
  349.4 142.9 %all-reduce.20.cloned.1.call-done = (bf16[512,256]{0,1:T(8,128)(2,1)}, bf16[512,512]{1,0:T(8,128)(2,1)}) async-done(((bf16[512,256]{0,1:T(8,128)(2,1)}, bf16[512,512]{1,0:T(8,128)(2,1)}), (bf16[512,256]{0,1:T(8,128)(2,1)}, bf16[512,512]{1,0:T(8,128)(2,1)})) %all-reduce.20.cloned.1.call-update) | async-done | bytes 786448 | tf_op jit(solution)/shard_map/psum | solution.py:11
  492.3 1.2 multiply_reduce_fusion.10
  493.5 5.4 convolution_subtract_fusion.3
  498.9 1.3 subtract_select_fusion.3
  500.2 3.5 dynamic_update_slice.20
  503.6 3.2 convert_select_fusion.2
  506.9 0.3 all-reduce.16.cloned.1.call-start
  507.1 2.8 multiply_reduce_fusion.4
  509.9 0.7 bitcast_dynamic-update-slice_fusion.3
  510.6 142.7 %all-reduce.18.cloned.1.call-done = (bf16[512,256]{0,1:T(8,128)(2,1)}, bf16[512,512]{1,0:T(8,128)(2,1)}) async-done(((bf16[512,256]{0,1:T(8,128)(2,1)}, bf16[512,512]{1,0:T(8,128)(2,1)}), (bf16[512,256]{0,1:T(8,128)(2,1)}, bf16[512,512]{1,0:T(8,128)(2,1)})) %all-reduce.18.cloned.1.call-update) | async-done | bytes 786448 | tf_op jit(solution)/shard_map/psum | solution.py:11
  653.3 1.2 multiply_reduce_fusion.9
  654.5 5.4 convolution_subtract_fusion.2
  659.9 1.2 subtract_select_fusion.2
  661.2 2.8 dynamic_update_slice.21
  664.0 3.2 convert_select_fusion.1
  667.3 0.0 all-reduce.14.cloned.1.call-start
  667.3 2.8 multiply_reduce_fusion.3
  670.1 0.7 bitcast_dynamic-update-slice_fusion.2
  670.8 142.9 %all-reduce.16.cloned.1.call-done = (bf16[512,256]{0,1:T(8,128)(2,1)}, bf16[512,512]{1,0:T(8,128)(2,1)}) async-done(((bf16[512,256]{0,1:T(8,128)(2,1)}, bf16[512,512]{1,0:T(8,128)(2,1)}), (bf16[512,256]{0,1:T(8,128)(2,1)}, bf16[512,512]{1,0:T(8,128)(2,1)})) %all-reduce.16.cloned.1.call-update) | async-done | bytes 786448 | tf_op jit(solution)/shard_map/psum | solution.py:11
  813.7 1.2 multiply_reduce_fusion.8
  814.9 5.4 convolution_subtract_fusion.1
  820.3 1.2 subtract_select_fusion.1
  821.6 2.8 dynamic_update_slice.22
  824.4 3.2 convert_select_fusion
  827.7 2.7 multiply_reduce_fusion.2
  830.4 0.7 bitcast_dynamic-update-slice_fusion.1
  831.1 143.6 %all-reduce.14.cloned.1.call-done = (bf16[512,256]{0,1:T(8,128)(2,1)}, bf16[512,512]{1,0:T(8,128)(2,1)}) async-done(((bf16[512,256]{0,1:T(8,128)(2,1)}, bf16[512,512]{1,0:T(8,128)(2,1)}), (bf16[512,256]{0,1:T(8,128)(2,1)}, bf16[512,512]{1,0:T(8,128)(2,1)})) %all-reduce.14.cloned.1.call-update) | async-done | bytes 786448 | tf_op jit(solution)/shard_map/psum | solution.py:11
  974.8 1.2 multiply_reduce_fusion.7
  976.0 5.4 convolution_subtract_fusion
  981.4 1.2 subtract_select_fusion
  982.6 2.8 dynamic_update_slice.23
  985.5 2.9 multiply_reduce_fusion.1
  988.4 1.8 copy.14
  990.2 64.9 %all-reduce = (f32[]{:T(128)}, f32[]{:T(128)}, f32[]{:T(128)}, f32[]{:T(128)}, f32[]{:T(128)}, /*index=5*/f32[]{:T(128)}) all-reduce(f32[]{:T(128)} %multiply_reduce_fusion.6, f32[]{:T(128)} %multiply_reduce_fusion.5, f32[]{:T(128)} %multiply_reduce_fusion.4, ...), channel_id=1, replica_groups=mesh['row'=8,'col'=16] {'row','col'}, use_global_device_ids=true, to_apply=%region_20.21 | all-reduce | flops 6 | bytes 48 | tf_op jit(solution)/shard_map/psum | solution.py:64
  1058.7 0.7 bitcast_dynamic-update-slice_fusion
  1059.4 2.6 copy.15
  1062.0 0.6 stack.55
  (20 shorter events, 0.1 us)
Async XLA Ops:
  7.2 9.6 copy-start
  7.2 163.0 %all-reduce.24.cloned.1.call-start = ((), (), s32[]{:S(2)}) async-start(), calls=%async_computation.5 | async-start | bytes 1572864 | tf_op jit(solution)/shard_map/psum | solution.py:11
  19.0 312.2 %all-reduce.22.cloned.1.call-start = ((), (), s32[]{:S(2)}) async-start(), calls=%async_computation.4 | async-start | bytes 1572864 | tf_op jit(solution)/shard_map/psum | solution.py:11
  180.9 6.2 copy-start.3
  184.2 308.1 %all-reduce.20.cloned.1.call-start = ((), (), s32[]{:S(2)}) async-start(), calls=%async_computation.3 | async-start | bytes 1572864 | tf_op jit(solution)/shard_map/psum | solution.py:11
  342.6 6.1 copy-start.6
  345.9 307.4 %all-reduce.18.cloned.1.call-start = ((), (), s32[]{:S(2)}) async-start(), calls=%async_computation.2 | async-start | bytes 1572864 | tf_op jit(solution)/shard_map/psum | solution.py:11
  503.6 6.3 copy-start.4
  506.9 306.8 %all-reduce.16.cloned.1.call-start = ((), (), s32[]{:S(2)}) async-start(), calls=%async_computation.1 | async-start | bytes 1572864 | tf_op jit(solution)/shard_map/psum | solution.py:11
  664.0 6.1 copy-start.5
  667.3 307.5 %all-reduce.14.cloned.1.call-start = ((), (), s32[]{:S(2)}) async-start(), calls=%async_computation | async-start | bytes 1572864 | tf_op jit(solution)/shard_map/psum | solution.py:11
  824.4 6.0 copy-start.7
  985.5 2.9 copy-start.1
  988.4 70.3 %copy-start.2 = (bf16[512,256]{0,1:T(8,128)(2,1)S(1)}, bf16[512,256]{0,1:T(8,128)(2,1)}, u32[]{:S(2)}) copy-start(bf16[512,256]{0,1:T(8,128)(2,1)} %get-tuple-element.12) | copy-start | bytes 786436
Sparse Core Ops, SparseCore 0:
  19.2 150.9 all-reduce.23
  184.3 146.8 all-reduce.21
  346.0 146.2 all-reduce.19
  507.0 146.2 all-reduce.17
  667.4 146.2 all-reduce.15
  827.8 146.9 all-reduce.13
where the time goes:
time: 1070 us
  waiting for transfers between devices  863 us (81%)
  blocking collectives  64.9 us (6%)
  matrix products  52.6 us (5%)
  other arithmetic  34.2 us (3%)
  local copies, waits for them, and re-layouts  32.1 us (3%)
  between operations  21.9 us (2%)
    psum x6, waiting for transfers between devices, broadcast(): return lax.psum(block, axis)  863 us
    psum x1, blocking collectives, on_device(): losses.append(lax.psum(partial_sum, ('row', 'col')) / total)  64.9 us
    dot_general x6, matrix products, on_device(): jnp.dot(kernel, shared_step, preferred_element_type=jnp.float32)  32.4 us
  transfers between devices with their start and end apart: 6, of which 6 were waited for; matrix products, arithmetic and copies ran while one was open for 2% of the time, Pallas kernels for 0%

commit v1 on v0

v1 whole, which is shorter than its diff:
```python
import jax
import jax.numpy as jnp
from jax import lax
from jax.experimental import pallas as pl
from jax.experimental.pallas import tpu as pltpu
from jax.sharding import PartitionSpec as P

RIDGE = 1.0
MESH = pl.DeviceIdType.MESH
ROUNDS = 6
BLK = 512
F = 512
K = 256
GAMMA = 2.0 / F
NT = (((1,), (1,)), ((), ()))
NN = (((1,), (0,)), ((), ()))
COPIES = 19


def coords():
    row = lax.axis_index("row")
    col = lax.axis_index("col")
    return (lax.div(col, 4), lax.div(row, 2), lax.rem(col, 4), lax.rem(row, 2))


def device(x, y, z, core):
    return (y * 2 + core, x * 4 + z)


def shifted(me, axis, delta):
    c = list(me)
    c[axis] = lax.rem(c[axis] + delta, 4)
    return device(*c)


def owner_of(block):
    d = block >> 2
    row, col = d >> 4, d & 15
    return (col >> 2, row >> 1, col & 3, row & 1), block & 3


def pick(slots, index):
    low = lax.select_n(index == 1, slots[0], slots[1])
    high = lax.select_n(index == 3, slots[2], slots[3])
    return lax.select_n(index >= 2, low, high)


class Chunk:
    def __init__(self, index, r, me, plan_ref, src, dst, bufs, sems):
        self.i, self.r, self.me = index, r, me
        self.src, self.dst = src, dst
        self.snd, self.cb, self.s0, self.ra, self.rb, self.rl, self.rr, self.s1, self.b2, self.b3 = (
            b.at[r] for b in bufs
        )
        self.ss, self.rs = sems
        self.owner, self.blk = owner_of(plan_ref[r])
        color = index % 3
        self.ax = [(color + j) % 3 for j in range(3)]
        self.a, self.b, self.c = (me[t] for t in self.ax)
        self.oa, self.ob, self.oc = (self.owner[t] for t in self.ax)
        self.core, self.ocore = me[3], self.owner[3]
        self.copies = {}

    def send(self, k, src, dst, dev):
        c = pltpu.make_async_remote_copy(
            src_ref=src, dst_ref=dst, send_sem=self.ss.at[self.i, k], recv_sem=self.rs.at[self.i, k],
            device_id=dev, device_id_type=MESH,
        )
        c.start()
        self.copies[k] = c

    def got(self, *ks):
        for k in ks:
            self.copies[k].wait_recv()

    def partner(self):
        x, y, z, core = self.me
        return device(x, y, z, 1 - core)

    def step0(self):
        self.snd[...] = self.src[self.blk, pl.ds(pl.multiple_of((1 - self.core) * 256, 256), 256), :]
        self.send(0, self.snd, self.cb, self.partner())

    def step1(self):
        self.got(0)
        own = self.src[self.blk, pl.ds(pl.multiple_of(self.core * 256, 256), 256), :]
        self.s0[...] = lax.select_n(self.ocore == self.core, self.cb[...], own)
        opp = lax.rem(self.a + 2, 4) * 64
        self.send(1, self.s0.at[pl.ds(pl.multiple_of(opp, 64), 32)], self.ra, shifted(self.me, self.ax[0], 1))
        self.send(2, self.s0.at[pl.ds(pl.multiple_of(opp + 32, 32), 32)], self.rb, shifted(self.me, self.ax[0], 3))

    def step2(self):
        self.got(1, 2)
        right = pl.multiple_of(lax.rem(self.a + 1, 4) * 64, 64)
        left = pl.multiple_of(lax.rem(self.a + 3, 4) * 64, 64)
        d = (self.oa - self.a) & 3
        ra = self.s0.at[pl.ds(right, 32)]
        ra[...] = lax.select_n(d == 3, ra[...], self.ra[...])
        lb = self.s0.at[pl.ds(pl.multiple_of(left + 32, 32), 32)]
        lb[...] = lax.select_n(d == 1, lb[...], self.rb[...])
        self.send(3, self.s0.at[pl.ds(right, 64)], self.rl, shifted(self.me, self.ax[0], 1))
        self.send(4, self.s0.at[pl.ds(left, 64)], self.rr, shifted(self.me, self.ax[0], 3))

    def step3(self):
        self.got(3, 4)
        d = (self.oa - self.a) & 3
        mine = self.a * 64
        va = lax.select_n(d == 1, self.rl[0:32], self.rr[0:32])
        self.s1[0:32] = lax.select_n(d == 0, va, self.s0[pl.ds(pl.multiple_of(mine, 64), 32), :])
        vb = lax.select_n(d == 3, self.rr[32:64], self.rl[32:64])
        self.s1[32:64] = lax.select_n(d == 0, vb, self.s0[pl.ds(pl.multiple_of(mine + 32, 32), 32), :])
        self.b2[self.b] = self.s1[pl.ds(pl.multiple_of(self.b * 16, 16), 16), :]
        for t in (1, 2, 3):
            q = lax.rem(self.b + t, 4) * 16
            self.send(4 + t, self.s1.at[pl.ds(pl.multiple_of(q, 16), 16)], self.b2.at[self.b],
                      shifted(self.me, self.ax[1], t))

    def step4(self):
        self.got(5, 6, 7)
        self.b3[self.c] = pick(self.b2, self.ob)
        for t in (1, 2, 3):
            self.send(7 + t, self.b3.at[self.c], self.b3.at[self.c], shifted(self.me, self.ax[2], t))

    def rows(self, start, count):
        return self.dst.at[self.r, pl.ds(pl.multiple_of(self.core * 256 + start, min(count, 64)), count)]

    def step5(self):
        self.got(8, 9, 10)
        here = self.rows(self.a * 64 + self.b * 16, 16)
        here[...] = pick(self.b3, self.oc)
        for t in (1, 2, 3):
            self.send(10 + t, here, here, shifted(self.me, self.ax[1], t))

    def step6(self):
        self.got(11, 12, 13)
        here = self.rows(self.a * 64, 64)
        self.send(14, here, here, shifted(self.me, self.ax[0], 1))
        self.send(15, here, here, shifted(self.me, self.ax[0], 3))

    def step7(self):
        self.got(14, 15)
        fa = self.rows(lax.rem(self.a + 3, 4) * 64, 32)
        fb = self.rows(lax.rem(self.a + 1, 4) * 64 + 32, 32)
        self.send(16, fa, fa, shifted(self.me, self.ax[0], 1))
        self.send(17, fb, fb, shifted(self.me, self.ax[0], 3))

    def step8(self):
        self.got(16, 17)
        here = self.dst.at[self.r, pl.ds(pl.multiple_of(self.core * 256, 256), 256)]
        self.send(18, here, here, self.partner())

    def step9(self):
        self.got(18)

    def drain(self):
        for c in self.copies.values():
            c.wait_send()


STEPS = 10


def make_chunks(me, plan_ref, pts, tgt, outp, outt, bufp, buft, ss, rs):
    order = [("p", 0), ("p", 1), ("p", 2), ("p", 3), ("p", 4), ("p", 5),
             ("t", 0), ("t", 1), ("t", 2), ("t", 3), ("t", 4), ("t", 5)]
    chunks = []
    for i, (kind, r) in enumerate(order):
        if kind == "p":
            chunks.append(Chunk(i, r, me, plan_ref, pts, outp, bufp, (ss, rs)))
        else:
            chunks.append(Chunk(i, r, me, plan_ref, tgt, outt, buft, (ss, rs)))
    return chunks


def greet(peers):
    barrier = pltpu.get_barrier_semaphore()
    for dev in peers:
        pl.semaphore_signal(barrier, inc=1, device_id=dev, device_id_type=MESH)
    pl.semaphore_wait(barrier, len(peers))


def gather_kernel(plan_ref, pts, tgt, outp, outt, *scratch):
    bufp, buft, ss, rs = scratch[:10], scratch[10:20], scratch[20], scratch[21]
    me = coords()
    x, y, z, core = me
    greet([device(x, y, z, 1 - core)] + [shifted(me, ax, t) for ax in range(3) for t in (1, 2, 3)])
    chunks = make_chunks(me, plan_ref, pts, tgt, outp, outt, bufp, buft, ss, rs)
    batches = [chunks[3 * b:3 * b + 3] for b in range(4)]
    for tau in range(STEPS + 3):
        for b in range(4):
            s = tau - b
            if 0 <= s < STEPS:
                for ch in batches[b]:
                    getattr(ch, f"step{s}")()
    for ch in chunks:
        ch.drain()


def buffers(width, dtype):
    shapes = [(256,), (256,), (256,), (32,), (32,), (64,), (64,), (64,), (4, 16), (4, 16)]
    return [pltpu.VMEM((ROUNDS,) + s + (width,), dtype) for s in shapes]


def vm():
    return pl.BlockSpec(memory_space=pltpu.VMEM)


def sm():
    return pl.BlockSpec(memory_space=pltpu.SMEM)


def row_norm(block):
    sq = jnp.square(block.astype(jnp.float32))
    col = GAMMA * jnp.sum(sq, axis=1, keepdims=True)
    return col, jnp.transpose(jnp.broadcast_to(col, (block.shape[0], 128)))[0:1, :]


def kmat(x, xcol, b, brow):
    inner = lax.dot_general(x, b, NT, preferred_element_type=jnp.float32)
    return jnp.exp((2.0 * GAMMA) * inner - (xcol + brow)).astype(jnp.bfloat16)


def mm(a, b):
    return lax.dot_general(a, b, NN, preferred_element_type=jnp.float32)


def split(v):
    hi = v.astype(jnp.bfloat16)
    return hi, (v - hi.astype(jnp.float32)).astype(jnp.bfloat16)


def compute_kernel(plan_ref, pts, tgt, bp, bt, minv, res, steps_out, part, xcol, brow, bcol, steps):
    row = lax.axis_index("row")
    col = lax.axis_index("col")
    first = (row * 16 + col) * 4

    def norms(q, _):
        xcol[q] = row_norm(pts[q])[0]
        res[q] = tgt[q]
        return 0

    lax.fori_loop(0, 4, norms, 0)

    def block_norms(r, _):
        c, w = row_norm(bp[r])
        bcol[r] = c
        brow[r] = w
        return 0

    lax.fori_loop(0, ROUNDS, block_norms, 0)
    part[...] = jnp.zeros_like(part)

    def one_round(r, _):
        def earlier(s, y):
            k = kmat(bp[r], bcol[r], bp[s], brow[s])
            same = jnp.where(plan_ref[s] == plan_ref[r], RIDGE, 0.0)
            return y - mm(k, steps_out[s]) - same * steps[s]

        y = lax.fori_loop(0, r, earlier, bt[r])
        yh, yl = split(y)
        mh, ml = split(minv[r])
        step = mm(mh, yh) + (mm(mh, yl) + mm(ml, yh))
        steps[r] = step
        steps_out[r] = step.astype(jnp.bfloat16)

        def update(q, acc):
            k = kmat(pts[q], xcol[q], bp[r], brow[r])
            mine = jnp.where(plan_ref[r] == first + q, RIDGE, 0.0)
            new = res[q] - mm(k, steps_out[r]) - mine * steps[r]
            res[q] = new
            return acc + jnp.sum((new * new).reshape(64, 8, K), axis=0)

        acc = lax.fori_loop(0, 4, update, jnp.zeros((8, K), jnp.float32))
        part[r] = acc[:, :128] + acc[:, 128:]
        return 0

    lax.fori_loop(0, ROUNDS, one_round, 0)


def loss_kernel(total, part, out, mine, g1, mid, g2, ss1, rs1, ss2, rs2):
    me = coords()
    x, y, z, core = me
    near, far = [], []
    for t in range(1, 8):
        v = lax.rem(x * 2 + core + t, 8)
        near.append(device(lax.div(v, 2), y, z, lax.rem(v, 2)))
    for t in range(1, 16):
        v = lax.rem(y * 4 + z + t, 16)
        far.append(device(x, lax.div(v, 4), lax.rem(v, 4), core))
    greet(near + far)
    here1, here2 = x * 2 + core, y * 4 + z
    mine[...] = jnp.zeros_like(mine)
    for r in range(ROUNDS):
        mine[r:r + 1, :] = jnp.sum(part[r], axis=0, keepdims=True)
    g1[here1] = mine[...]
    c1 = []
    for t, dev in enumerate(near):
        c = pltpu.make_async_remote_copy(mine, g1.at[here1], ss1.at[t], rs1.at[t], device_id=dev, device_id_type=MESH)
        c.start()
        c1.append(c)
    for c in c1:
        c.wait_recv()
    mid[...] = jnp.sum(g1[...], axis=0)
    g2[here2] = mid[...]
    c2 = []
    for t, dev in enumerate(far):
        c = pltpu.make_async_remote_copy(mid, g2.at[here2], ss2.at[t], rs2.at[t], device_id=dev, device_id_type=MESH)
        c.start()
        c2.append(c)
    for c in c2:
        c.wait_recv()
    whole = jnp.sum(g2[...], axis=0)
    for r in range(ROUNDS):
        out[r] = jnp.sum(whole[r:r + 1, :]) * (1.0 / total)
    for c in c1 + c2:
        c.wait_send()


def on_device(points, targets, plan, block_inverse):
    rows = points.shape[0]
    total = rows * 128 * targets.shape[1]
    pts = points.reshape(4, BLK, F)
    tgt = targets.reshape(4, BLK, K)
    bp, bt = pl.pallas_call(
        gather_kernel,
        out_shape=(jax.ShapeDtypeStruct((ROUNDS, BLK, F), jnp.bfloat16),
                   jax.ShapeDtypeStruct((ROUNDS, BLK, K), jnp.float32)),
        in_specs=[sm(), vm(), vm()],
        out_specs=(vm(), vm()),
        scratch_shapes=buffers(F, jnp.bfloat16) + buffers(K, jnp.float32)
        + [pltpu.SemaphoreType.DMA((12, COPIES)), pltpu.SemaphoreType.DMA((12, COPIES))],
        compiler_params=pltpu.CompilerParams(collective_id=0, has_side_effects=True, vmem_limit_bytes=60 << 20),
        name="gather_blocks",
    )(plan, pts, tgt)
    res, steps, part = pl.pallas_call(
        compute_kernel,
        out_shape=(jax.ShapeDtypeStruct((4, BLK, K), jnp.float32),
                   jax.ShapeDtypeStruct((ROUNDS, BLK, K), jnp.bfloat16),
                   jax.ShapeDtypeStruct((ROUNDS, 8, 128), jnp.float32)),
        in_specs=[sm(), vm(), vm(), vm(), vm(), vm()],
        out_specs=(vm(), vm(), vm()),
        scratch_shapes=[pltpu.VMEM((4, BLK, 1), jnp.float32), pltpu.VMEM((ROUNDS, 1, BLK), jnp.float32),
                        pltpu.VMEM((ROUNDS, BLK, 1), jnp.float32), pltpu.VMEM((ROUNDS, BLK, K), jnp.float32)],
        compiler_params=pltpu.CompilerParams(vmem_limit_bytes=60 << 20),
        name="solve_update",
    )(plan, pts, tgt, bp, bt, block_inverse)
    losses = pl.pallas_call(
        lambda *a: loss_kernel(float(total), *a),
        out_shape=jax.ShapeDtypeStruct((ROUNDS,), jnp.float32),
        in_specs=[vm()],
        out_specs=sm(),
        scratch_shapes=[pltpu.VMEM((8, 128), jnp.float32), pltpu.VMEM((8, 8, 128), jnp.float32),
                        pltpu.VMEM((8, 128), jnp.float32), pltpu.VMEM((16, 8, 128), jnp.float32),
                        pltpu.SemaphoreType.DMA((7,)), pltpu.SemaphoreType.DMA((7,)),
                        pltpu.SemaphoreType.DMA((15,)), pltpu.SemaphoreType.DMA((15,))],
        compiler_params=pltpu.CompilerParams(collective_id=1, has_side_effects=True),
        name="sum_losses",
    )(part)
    return res.reshape(rows, K), steps, losses


def solution(mesh):
    placed = (P(("row", "col"), None), P(("row", "col"), None), P(), P())
    return jax.shard_map(
        on_device,
        mesh=mesh,
        in_specs=placed,
        out_specs=(P(("row", "col"), None), P(), P()),
        check_vma=False,
    )
```

time: 1070 us -> 121 us (0.11)
  waiting for transfers between devices: 863 us -> 0 us
  Pallas kernels: 0 us -> 119 us
  blocking collectives: 64.9 us -> 0 us
  matrix products: 52.6 us -> 0 us
  other arithmetic: 34.2 us -> 0 us
  local copies, waits for them, and re-layouts: 32.1 us -> 1.14 us
  between operations: 21.9 us -> 0.65 us
    psum x6 -> x0, waiting for transfers between devices: 863 us -> none  [broadcast(): return lax.psum(block, axis)]
    pallas_call x0 -> x3, Pallas kernels: none -> 119 us  [the longest x1 63.5 us: on_device(): pl.pallas_call(gather_kernel, out_shape=(jax.ShapeDtypeStruct((ROUNDS, BL...]
    psum x1 -> x0, blocking collectives: 64.9 us -> none  [on_device(): losses.append(lax.psum(partial_sum, ('row', 'col')) / total)]
    dot_general x12 -> x0, matrix products: 52.6 us -> none  [the longest x6 32.4 us: on_device(): jnp.dot(kernel, shared_step, preferred_element_type=jnp.float32)]
    reduce_sum x13 -> x0, other arithmetic: 24.4 us -> none  [the longest x6 16.6 us: on_device(): partial_sum = jnp.sum(residual * residual)]
    dynamic_update_slice x6 -> x0, local copies, waits for them, and re-layouts: 18.3 us -> none  [on_device(): residual = lax.dynamic_update_slice_in_dim(residual, owned, offset, 0)]
  transfers between devices with their start and end apart: 6 -> 0, of which waited for: 6 -> 0; matrix products, arithmetic and copies ran while one was open for 2% -> 0% of each run, Pallas kernels for 0% -> 0%
where the time goes in v1:
time: 121 us
  Pallas kernels  119 us (98%)
    pallas_call x1, Pallas kernels, on_device(): pl.pallas_call(gather_kernel, out_shape=(jax.ShapeDtypeStruct((ROUNDS, BL...  63.5 us
    pallas_call x1, Pallas kernels, on_device(): pl.pallas_call(compute_kernel, out_shape=(jax.ShapeDtypeStruct((4, BLK, K...  44.3 us
    pallas_call x1, Pallas kernels, on_device(): pl.pallas_call(lambda *a: loss_kernel(float(total), *a), out_shape=jax.Sh...  11.3 us

profile of v1, /device:TPU:1, one launch (start us, length us, event | category | flops | bytes accessed | tf_op | source)
XLA Modules:
  0.0 120.9 jit_solution(2625203259803957345)
XLA Ops:
  0.6 63.5 %gather_blocks.1 = (bf16[6,512,512]{2,1,0:T(8,128)(2,1)}, f32[6,512,256]{2,1,0:T(8,128)}) custom-call(s32[6]{0:T(128)} %plan_ref.3, bf16[4,512,512]{2,1,0:T(8,128)(2,1)} %bitcast.3, f32[4,512,256]{2,1,0:T(8,128)} %bitcast.5), custom_call_target="tpu_custom_call" | custom-call | tf_op jit(solution)/shard_map/gather_blocks/pallas_call | solution.py:324
  64.1 44.3 %solve_update.1 = (f32[4,512,256]{2,1,0:T(8,128)}, bf16[6,512,256]{2,1,0:T(8,128)(2,1)}, f32[6,8,128]{2,1,0:T(8,128)}) custom-call(s32[6]{0:T(128)} %plan_ref.3, bf16[4,512,512]{2,1,0:T(8,128)(2,1)} %bitcast.4, f32[4,512,256]{2,1,0:T(8,128)} %bitcast.6, bf16[6,512,512]{2,1,0:T(8,128)(2,1)} %get-tuple-element.8.bp, f32[6,512,256]{2,1,0:T(8,128)} %get-tuple-element.9.bt, ...), custom_call_target="tpu_custom_call" | custom-call | tf_op jit(solution)/shard_map/solve_update/pallas_call | solution.py:335
  108.4 11.3 %sum_losses.1 = f32[6]{0:T(128)} custom-call(f32[6,8,128]{2,1,0:T(8,128)} %get-tuple-element.12.a_0_), custom_call_target="tpu_custom_call" | custom-call | tf_op jit(solution)/shard_map/sum_losses/pallas_call | solution.py:347
  119.8 1.1 copy.8

commit v2 on v1

v2 whole, which is shorter than its diff:
```python
import jax
import jax.numpy as jnp
from jax import lax
from jax.experimental import pallas as pl
from jax.experimental.pallas import tpu as pltpu
from jax.sharding import PartitionSpec as P

RIDGE = 1.0
MESH = pl.DeviceIdType.MESH
ROUNDS = 6
BLK = 512
F = 512
K = 256
GAMMA = 2.0 / F
NT = (((1,), (1,)), ((), ()))
NN = (((1,), (0,)), ((), ()))
COPIES = 19
LOG2E = 1.4426950408889634


def coords():
    row = lax.axis_index("row")
    col = lax.axis_index("col")
    return (lax.div(col, 4), lax.div(row, 2), lax.rem(col, 4), lax.rem(row, 2))


def device(x, y, z, core):
    return (y * 2 + core, x * 4 + z)


def shifted(me, axis, delta):
    c = list(me)
    c[axis] = lax.rem(c[axis] + delta, 4)
    return device(*c)


def owner_of(block):
    d = block >> 2
    row, col = d >> 4, d & 15
    return (col >> 2, row >> 1, col & 3, row & 1), block & 3


def pick(slots, index):
    low = lax.select_n(index == 1, slots[0], slots[1])
    high = lax.select_n(index == 3, slots[2], slots[3])
    return lax.select_n(index >= 2, low, high)


class Chunk:
    def __init__(self, index, color, r, cols, me, plan_ref, src, dst, bufs, sems):
        self.i, self.r, self.me, self.cols = index, r, me, cols
        self.src, self.dst = src, dst
        snd, cb, s0, ra, rb, rl, rr, s1, b2, b3 = bufs
        self.snd, self.cb, self.s0, self.ra, self.rb, self.rl, self.rr, self.s1 = (
            b.at[r, :, cols] for b in (snd, cb, s0, ra, rb, rl, rr, s1)
        )
        self.b2, self.b3 = b2.at[r, :, :, cols], b3.at[r, :, :, cols]
        self.ss, self.rs = sems
        self.owner, self.blk = owner_of(plan_ref[r])
        self.ax = [(color + j) % 3 for j in range(3)]
        self.a, self.b, self.c = (me[t] for t in self.ax)
        self.oa, self.ob, self.oc = (self.owner[t] for t in self.ax)
        self.core, self.ocore = me[3], self.owner[3]
        self.copies = {}

    def send(self, k, src, dst, dev):
        c = pltpu.make_async_remote_copy(
            src_ref=src, dst_ref=dst, send_sem=self.ss.at[self.i, k], recv_sem=self.rs.at[self.i, k],
            device_id=dev, device_id_type=MESH,
        )
        c.start()
        self.copies[k] = c

    def got(self, *ks):
        for k in ks:
            self.copies[k].wait_recv()

    def partner(self):
        x, y, z, core = self.me
        return device(x, y, z, 1 - core)

    def half(self, core):
        return self.src[self.blk, pl.ds(pl.multiple_of(core * 256, 256), 256), self.cols]

    def step0(self):
        self.snd[...] = self.half(1 - self.core)
        self.send(0, self.snd, self.cb, self.partner())

    def step1(self):
        self.got(0)
        self.s0[...] = lax.select_n(self.ocore == self.core, self.cb[...], self.half(self.core))
        opp = lax.rem(self.a + 2, 4) * 64
        self.send(1, self.s0.at[pl.ds(pl.multiple_of(opp, 64), 32)], self.ra, shifted(self.me, self.ax[0], 1))
        self.send(2, self.s0.at[pl.ds(pl.multiple_of(opp + 32, 32), 32)], self.rb, shifted(self.me, self.ax[0], 3))

    def step2(self):
        self.got(1, 2)
        right = pl.multiple_of(lax.rem(self.a + 1, 4) * 64, 64)
        left = pl.multiple_of(lax.rem(self.a + 3, 4) * 64, 64)
        d = (self.oa - self.a) & 3
        ra = self.s0.at[pl.ds(right, 32)]
        ra[...] = lax.select_n(d == 3, ra[...], self.ra[...])
        lb = self.s0.at[pl.ds(pl.multiple_of(left + 32, 32), 32)]
        lb[...] = lax.select_n(d == 1, lb[...], self.rb[...])
        self.send(3, self.s0.at[pl.ds(right, 64)], self.rl, shifted(self.me, self.ax[0], 1))
        self.send(4, self.s0.at[pl.ds(left, 64)], self.rr, shifted(self.me, self.ax[0], 3))

    def step3(self):
        self.got(3, 4)
        d = (self.oa - self.a) & 3
        mine = self.a * 64
        va = lax.select_n(d == 1, self.rl[0:32], self.rr[0:32])
        self.s1[0:32] = lax.select_n(d == 0, va, self.s0[pl.ds(pl.multiple_of(mine, 64), 32), :])
        vb = lax.select_n(d == 3, self.rr[32:64], self.rl[32:64])
        self.s1[32:64] = lax.select_n(d == 0, vb, self.s0[pl.ds(pl.multiple_of(mine + 32, 32), 32), :])
        self.b2[self.b] = self.s1[pl.ds(pl.multiple_of(self.b * 16, 16), 16), :]
        for t in (1, 2, 3):
            q = lax.rem(self.b + t, 4) * 16
            self.send(4 + t, self.s1.at[pl.ds(pl.multiple_of(q, 16), 16)], self.b2.at[self.b],
                      shifted(self.me, self.ax[1], t))

    def step4(self):
        self.got(5, 6, 7)
        self.b3[self.c] = pick(self.b2, self.ob)
        for t in (1, 2, 3):
            self.send(7 + t, self.b3.at[self.c], self.b3.at[self.c], shifted(self.me, self.ax[2], t))

    def rows(self, start, count):
        return self.dst.at[self.r, pl.ds(pl.multiple_of(self.core * 256 + start, min(count, 64)), count), self.cols]

    def step5(self):
        self.got(8, 9, 10)
        here = self.rows(self.a * 64 + self.b * 16, 16)
        here[...] = pick(self.b3, self.oc)
        for t in (1, 2, 3):
            self.send(10 + t, here, here, shifted(self.me, self.ax[1], t))

    def step6(self):
        self.got(11, 12, 13)
        here = self.rows(self.a * 64, 64)
        self.send(14, here, here, shifted(self.me, self.ax[0], 1))
        self.send(15, here, here, shifted(self.me, self.ax[0], 3))

    def step7(self):
        self.got(14, 15)
        fa = self.rows(lax.rem(self.a + 3, 4) * 64, 32)
        fb = self.rows(lax.rem(self.a + 1, 4) * 64 + 32, 32)
        self.send(16, fa, fa, shifted(self.me, self.ax[0], 1))
        self.send(17, fb, fb, shifted(self.me, self.ax[0], 3))

    def step8(self):
        self.got(16, 17)
        here = self.rows(0, 256)
        self.send(18, here, here, self.partner())

    def step9(self):
        self.got(18)

    def drain(self):
        for c in self.copies.values():
            c.wait_send()


STEPS = 10
WHOLE = slice(None)
BATCHES = [
    [("p", 0, slice(0, 128)), ("p", 0, slice(128, 256)), ("p", 0, slice(256, 512))],
    [("p", 1, WHOLE), ("p", 2, WHOLE), ("p", 3, WHOLE)],
    [("p", 4, WHOLE), ("p", 5, WHOLE), ("t", 0, WHOLE)],
    [("t", 1, WHOLE), ("t", 2, WHOLE), ("t", 3, WHOLE)],
    [("t", 4, WHOLE), ("t", 5, WHOLE)],
]
CHUNKS = sum(len(b) for b in BATCHES)
WIRE = [1.7, 0.7, 1.4, 1.0, 1.0, 1.0, 1.4, 0.7, 1.7]
FLIGHT = [1.0, 2.7, 2.7, 2.7, 2.7, 2.7, 2.7, 2.7, 1.0]
ISSUE = [0.4, 0.4, 0.25, 0.2, 0.15, 0.15, 0.1, 0.1, 0.1, 0.05]


def plan_order(units):
    order, done, now = [], set(), 0.0
    free = {"core": 0.0, "ici": 0.0}
    following = [0] * len(BATCHES)
    ready = [0.0] * len(BATCHES)
    size = [0.5] + [1.0] * (len(BATCHES) - 1)
    left = dict(units)
    while True:
        steps = [(ready[b], b) for b in range(len(BATCHES)) if following[b] < STEPS]
        if not steps and not left:
            return order
        due = [(b, ready[b]) for _, b in steps if ready[b] <= now]
        if due:
            b = due[0][0]
            s = following[b]
            order.append(("step", b, s))
            now += ISSUE[s] * len(BATCHES[b]) / 3
            if s == STEPS - 1:
                done.update(("block", k, r) for k, r, _ in BATCHES[b])
            else:
                link = "core" if s in (0, 8) else "ici"
                start = max(now, free[link])
                free[link] = start + WIRE[s] * size[b]
                ready[b] = free[link] + FLIGHT[s]
            following[b] += 1
            continue
        name = next((n for n, (_, needs) in left.items() if all(d in done for d in needs)), None)
        if name is not None:
            order.append(name)
            now += left.pop(name)[0]
            done.add(name)
            continue
        now = min(t for t, _ in steps)


def work_units():
    units = {}
    for q in range(4):
        units[("xnorm", q)] = (0.3, [])
    for r in range(ROUNDS):
        units[("minv", r)] = (0.5, [])
    for r in range(ROUNDS):
        before = [("upd", r - 1)] if r else []
        units[("solve", r)] = (0.8 + 0.25 * r, [("block", "t", r), ("minv", r)]
                               + [("pair", r, s) for s in range(r)] + ([("solve", r - 1)] if r else []))
        units[("upd", r)] = (1.1, [("solve", r), ("own", r, 0), ("own", r, 1), ("block", "t", ROUNDS - 1)] + before)
    for r in range(ROUNDS):
        units[("bnorm", r)] = (0.4, [("block", "p", r)])
        for s in range(r):
            units[("pair", r, s)] = (0.4, [("bnorm", r), ("bnorm", s)])
        for h in range(2):
            units[("own", r, h)] = (0.75, [("bnorm", r), ("xnorm", 3)])
    return units


ORDER = plan_order(work_units())


def greet(peers):
    barrier = pltpu.get_barrier_semaphore()
    for dev in peers:
        pl.semaphore_signal(barrier, inc=1, device_id=dev, device_id_type=MESH)
    pl.semaphore_wait(barrier, len(peers))


def buffers(width, dtype):
    shapes = [(256,), (256,), (256,), (32,), (32,), (64,), (64,), (64,), (4, 16), (4, 16)]
    return [pltpu.VMEM((ROUNDS,) + s + (width,), dtype) for s in shapes]


def to_row(col):
    return jnp.transpose(jnp.broadcast_to(col, (col.shape[0], 128)))[0:1, :]


def norm(block):
    sq = jnp.square(block.astype(jnp.float32))
    return (GAMMA * LOG2E) * jnp.sum(sq, axis=1, keepdims=True)


def kmat(x, xcol, b, brow):
    inner = lax.dot_general(x, b, NT, preferred_element_type=jnp.float32)
    return jnp.exp2((2.0 * GAMMA * LOG2E) * inner - (xcol + brow)).astype(jnp.bfloat16)


def mm(a, b):
    return lax.dot_general(a, b, NN, preferred_element_type=jnp.float32)


def split(v):
    hi = v.astype(jnp.bfloat16)
    return hi, (v - hi.astype(jnp.float32)).astype(jnp.bfloat16)


def whole_kernel(total, plan_ref, pts_hbm, tgt_hbm, inv_hbm, res_hbm, steps_hbm, out, *scratch):
    bufp, buft = scratch[:10], scratch[10:20]
    (ss, rs, pts, res, bp, bt, minv, mh, ml, kown, kp1, kp2, kp3, kp4, kp5, xcol, bcol, brow, steps, sh, part,
     mine_loss, g1, mid, g2, ss1, rs1, ss2, rs2, local, msem, osem) = scratch[20:]
    kp = [None, kp1, kp2, kp3, kp4, kp5]
    me = coords()
    x, y, z, core = me
    first = (lax.axis_index("row") * 16 + lax.axis_index("col")) * 4
    loads = [pltpu.make_async_copy(pts_hbm, pts, local.at[0]), pltpu.make_async_copy(tgt_hbm, res, local.at[1])]
    for c in loads:
        c.start()
    fetch = [pltpu.make_async_copy(inv_hbm.at[r], minv.at[r % 2], msem.at[r]) for r in range(ROUNDS)]
    fetch[0].start()
    fetch[1].start()
    near, far, near_id, far_id = [], [], x * 2 + core, y * 4 + z
    for t in range(1, 8):
        v = lax.rem(near_id + t, 8)
        near.append(device(lax.div(v, 2), y, z, lax.rem(v, 2)))
    for t in range(1, 16):
        v = lax.rem(far_id + t, 16)
        far.append(device(x, lax.div(v, 4), lax.rem(v, 4), core))
    greet(near + far)
    for c in loads:
        c.wait()

    batches, index = [], 0
    for batch in BATCHES:
        made = []
        for color, (kind, r, cols) in enumerate(batch):
            src, dst, bufs = (pts, bp, bufp) if kind == "p" else (res, bt, buft)
            made.append(Chunk(index, color, r, cols, me, plan_ref, src, dst, bufs, (ss, rs)))
            index += 1
        batches.append(made)
    writes = []

    def do_minv(r):
        fetch[r].wait()
        mh[r], ml[r] = split(minv[r % 2])
        if r + 2 < ROUNDS:
            fetch[r + 2].start()

    def do_bnorm(r):
        c = norm(bp[r])
        bcol[r] = c
        brow[r] = to_row(c)

    def do_xnorm(q):
        xcol[q] = norm(pts[q])

    def do_pair(r, s):
        kp[r][:, s * BLK:(s + 1) * BLK] = kmat(bp[r], bcol[r], bp[s], brow[s])

    def do_own(r, h):
        def tile(q, _):
            kown[r, q] = kmat(pts[q], xcol[q], bp[r], brow[r])
            return 0

        lax.fori_loop(2 * h, 2 * h + 2, tile, 0)

    def do_solve(r):
        v = bt[r]
        for s in range(r):
            v = v - jnp.where(plan_ref[s] == plan_ref[r], RIDGE, 0.0) * steps[s]
        if r:
            v = v - mm(kp[r][...], sh[0:r * BLK, :])
        yh, yl = split(v)
        step = mm(mh[r], yh) + (mm(mh[r], yl) + mm(ml[r], yh))
        steps[r] = step
        sh[r * BLK:(r + 1) * BLK, :] = step.astype(jnp.bfloat16)

    def do_upd(r):
        def tile(q, acc):
            mine = jnp.where(plan_ref[r] == first + q, RIDGE, 0.0)
            new = res[q] - mm(kown[r, q], sh[r * BLK:(r + 1) * BLK, :]) - mine * steps[r]
            res[q] = new
            return acc + jnp.sum((new * new).reshape(64, 8, K), axis=0)

        acc = lax.fori_loop(0, 4, tile, jnp.zeros((8, K), jnp.float32))
        part[r:r + 1, :] = jnp.sum(acc[:, :128] + acc[:, 128:], axis=0, keepdims=True)
        c = pltpu.make_async_copy(sh.at[r * BLK:(r + 1) * BLK, :], steps_hbm.at[r], osem.at[r])
        c.start()
        writes.append(c)

    part[...] = jnp.zeros_like(part)
    todo = {"minv": do_minv, "bnorm": do_bnorm, "xnorm": do_xnorm, "pair": do_pair, "own": do_own,
            "solve": do_solve, "upd": do_upd}
    for item in ORDER:
        if item[0] == "step":
            for ch in batches[item[1]]:
                getattr(ch, f"step{item[2]}")()
        else:
            todo[item[0]](*item[1:])

    mine_loss[...] = part[...]
    g1[near_id] = part[...]
    c1 = []
    for t, dev in enumerate(near):
        c = pltpu.make_async_remote_copy(mine_loss, g1.at[near_id], ss1.at[t], rs1.at[t], device_id=dev, device_id_type=MESH)
        c.start()
        c1.append(c)
    c = pltpu.make_async_copy(res, res_hbm, osem.at[ROUNDS])
    c.start()
    writes.append(c)
    for c in c1:
        c.wait_recv()
    mid[...] = jnp.sum(g1[...], axis=0)
    g2[far_id] = mid[...]
    c2 = []
    for t, dev in enumerate(far):
        c = pltpu.make_async_remote_copy(mid, g2.at[far_id], ss2.at[t], rs2.at[t], device_id=dev, device_id_type=MESH)
        c.start()
        c2.append(c)
    for batch in batches:
        for ch in batch:
            ch.drain()
    for c in c2:
        c.wait_recv()
    whole = jnp.sum(g2[...], axis=0)
    for r in range(ROUNDS):
        out[r] = jnp.sum(whole[r:r + 1, :]) * (1.0 / total)
    for c in c1 + c2:
        c.wait_send()
    for c in writes:
        c.wait()


def on_device(points, targets, plan, block_inverse):
    rows = points.shape[0]
    total = float(rows * 128 * targets.shape[1])
    anywhere = pl.BlockSpec(memory_space=pl.ANY)
    smem = pl.BlockSpec(memory_space=pltpu.SMEM)
    f32, b16, dma = jnp.float32, jnp.bfloat16, pltpu.SemaphoreType.DMA
    res, steps, losses = pl.pallas_call(
        lambda *refs: whole_kernel(total, *refs),
        out_shape=(jax.ShapeDtypeStruct((4, BLK, K), f32), jax.ShapeDtypeStruct((ROUNDS, BLK, K), b16),
                   jax.ShapeDtypeStruct((ROUNDS,), f32)),
        in_specs=[smem, anywhere, anywhere, anywhere],
        out_specs=(anywhere, anywhere, smem),
        scratch_shapes=buffers(F, b16) + buffers(K, f32) + [
            dma((CHUNKS, COPIES)), dma((CHUNKS, COPIES)),
            pltpu.VMEM((4, BLK, F), b16), pltpu.VMEM((4, BLK, K), f32),
            pltpu.VMEM((ROUNDS, BLK, F), b16), pltpu.VMEM((ROUNDS, BLK, K), f32),
            pltpu.VMEM((2, BLK, BLK), f32), pltpu.VMEM((ROUNDS, BLK, BLK), b16), pltpu.VMEM((ROUNDS, BLK, BLK), b16),
            pltpu.VMEM((ROUNDS, 4, BLK, BLK), b16),
            *[pltpu.VMEM((BLK, r * BLK), b16) for r in range(1, ROUNDS)],
            pltpu.VMEM((4, BLK, 1), f32), pltpu.VMEM((ROUNDS, BLK, 1), f32), pltpu.VMEM((ROUNDS, 1, BLK), f32),
            pltpu.VMEM((ROUNDS, BLK, K), f32), pltpu.VMEM((ROUNDS * BLK, K), b16), pltpu.VMEM((8, 128), f32),
            pltpu.VMEM((8, 128), f32), pltpu.VMEM((8, 8, 128), f32), pltpu.VMEM((8, 128), f32),
            pltpu.VMEM((16, 8, 128), f32),
            dma((7,)), dma((7,)), dma((15,)), dma((15,)), dma((2,)), dma((ROUNDS,)), dma((ROUNDS + 1,)),
        ],
        compiler_params=pltpu.CompilerParams(collective_id=0, has_side_effects=True, vmem_limit_bytes=67043328),
        name="block_ridge",
    )(plan, points.reshape(4, BLK, F), targets.reshape(4, BLK, K), block_inverse)
    return res.reshape(rows, K), steps, losses


def solution(mesh):
    placed = (P(("row", "col"), None), P(("row", "col"), None), P(), P())
    return jax.shard_map(
        on_device,
        mesh=mesh,
        in_specs=placed,
        out_specs=(P(("row", "col"), None), P(), P()),
        check_vma=False,
    )
```

time: 121 us -> 95 us (0.79)
  Pallas kernels: 119 us -> 89.4 us
  local copies, waits for them, and re-layouts: 1.14 us -> 4.82 us
    pallas_call x3 -> x1, Pallas kernels: 119 us -> 89.4 us  [on_device(): pl.pallas_call(lambda *refs: whole_kernel(total, *refs), out_shape=(jax.S...]
    unnamed x1 -> x7, local copies, waits for them, and re-layouts: 1.14 us -> 4.82 us
where the time goes in v2:
time: 95 us; the launch traced here: 94.9 us
  Pallas kernels  89.4 us (94%)
  local copies, waits for them, and re-layouts  4.82 us (5%)
    pallas_call x1, Pallas kernels, on_device(): pl.pallas_call(lambda *refs: whole_kernel(total, *refs), out_shape=(jax.S...  89.4 us
    unnamed x7, local copies, waits for them, and re-layouts  4.82 us

profile of v2, /device:TPU:1, one launch (start us, length us, event | category | flops | bytes accessed | tf_op | source)
XLA Modules:
  0.0 94.9 jit_solution(369318941010467557)
XLA Ops:
  0.6 89.4 %block_ridge.1 = (f32[4,512,256]{2,1,0:T(8,128)}, bf16[6,512,256]{2,1,0:T(8,128)(2,1)}, f32[6]{0:T(128)}) custom-call(s32[6]{0:T(128)} %refs_0_.1, bf16[4,512,512]{2,1,0:T(8,128)(2,1)} %bitcast.4, f32[4,512,256]{2,1,0:T(8,128)} %bitcast.5, f32[6,512,512]{2,1,0:T(8,128)} %refs_3_.1), custom_call_target="tpu_custom_call" | custom-call | tf_op jit(solution)/shard_map/block_ridge/pallas_call | solution.py:404
  90.0 0.0 copy-start
  90.0 3.2 %copy.10 = f32[2048,256]{1,0:T(8,128)} copy(f32[2048,256]{1,0:T(8,128)} %bitcast.3) | data formatting | bytes 4194304
  93.2 0.0 copy-done
  93.2 0.0 copy-start.1
  93.2 1.1 %copy.11 = bf16[6,512,256]{2,1,0:T(8,128)(2,1)} copy(bf16[6,512,256]{2,1,0:T(8,128)(2,1)S(1)} %copy-done) | data formatting | bytes 3145728
  94.3 0.0 copy-done.1
  94.3 0.5 copy.12
Async XLA Ops:
  90.0 3.2 %copy-start = (bf16[6,512,256]{2,1,0:T(8,128)(2,1)S(1)}, bf16[6,512,256]{2,1,0:T(8,128)(2,1)}, u32[]{:S(2)}) copy-start(bf16[6,512,256]{2,1,0:T(8,128)(2,1)} %get-tuple-element.13) | copy-start | bytes 4718596
  93.2 1.1 %copy-start.1 = (f32[6]{0:T(128)S(1)}, f32[6]{0:T(128)}, u32[]{:S(2)}) copy-start(f32[6]{0:T(128)} %get-tuple-element.14) | copy-start | bytes 76

commit v3 on v2

v3 whole, which is shorter than its diff:
```python
import jax
import jax.numpy as jnp
from jax import lax
from jax.experimental import pallas as pl
from jax.experimental.pallas import tpu as pltpu
from jax.sharding import PartitionSpec as P

RIDGE = 1.0
MESH = pl.DeviceIdType.MESH
ROUNDS = 6
BLK = 512
F = 512
K = 256
GAMMA = 2.0 / F
NT = (((1,), (1,)), ((), ()))
NN = (((1,), (0,)), ((), ()))
LOG2E = 1.4426950408889634


def coords():
    row = lax.axis_index("row")
    col = lax.axis_index("col")
    return (lax.div(col, 4), lax.div(row, 2), lax.rem(col, 4), lax.rem(row, 2))


def device(x, y, z, core):
    return (y * 2 + core, x * 4 + z)


def shifted(me, axis, delta):
    c = list(me)
    c[axis] = lax.rem(c[axis] + delta, 4)
    return device(*c)


def owner_of(block):
    d = block >> 2
    row, col = d >> 4, d & 15
    return (col >> 2, row >> 1, col & 3, row & 1), block & 3


def pick(slots, index):
    low = lax.select_n(index == 1, slots[0], slots[1])
    high = lax.select_n(index == 3, slots[2], slots[3])
    return lax.select_n(index >= 2, low, high)


class Chunk:
    def __init__(self, color, r, cols, me, plan_ref, src, dst, bufs, sems):
        self.r, self.me, self.cols = r, me, cols
        self.src, self.dst = src, dst
        snd, cb, s0, b1, s1, b2, b3 = bufs
        self.snd, self.cb, self.s0, self.s1 = (b.at[r, :, cols] for b in (snd, cb, s0, s1))
        self.b1, self.b2, self.b3 = (b.at[r, :, :, cols] for b in (b1, b2, b3))
        self.ra, self.rb = self.b1.at[0, 0:32], self.b1.at[0, 32:64]
        self.rl, self.rr = self.b1.at[1], self.b1.at[2]
        self.ssem, self.rsem = sems
        self.owner, self.blk = owner_of(plan_ref[r])
        self.ax = [(color + j) % 3 for j in range(3)]
        self.a, self.b, self.c = (me[t] for t in self.ax)
        self.oa, self.ob, self.oc = (self.owner[t] for t in self.ax)
        self.core, self.ocore = me[3], self.owner[3]
        self.stage = 0

    def send(self, src, dst, dev):
        pltpu.make_async_remote_copy(
            src_ref=src, dst_ref=dst, send_sem=self.ssem, recv_sem=self.rsem.at[self.stage],
            device_id=dev, device_id_type=MESH,
        ).start()

    def partner(self):
        x, y, z, core = self.me
        return device(x, y, z, 1 - core)

    def half(self, core):
        return self.src[self.blk, pl.ds(pl.multiple_of(core * 256, 256), 256), self.cols]

    def stage_half(self):
        self.snd[...] = self.half(1 - self.core)

    def step0(self):
        self.send(self.snd, self.cb, self.partner())

    def step1(self):
        self.s0[...] = lax.select_n(self.ocore == self.core, self.cb[...], self.half(self.core))
        opp = lax.rem(self.a + 2, 4) * 64
        self.send(self.s0.at[pl.ds(pl.multiple_of(opp, 64), 32)], self.ra, shifted(self.me, self.ax[0], 1))
        self.send(self.s0.at[pl.ds(pl.multiple_of(opp + 32, 32), 32)], self.rb, shifted(self.me, self.ax[0], 3))

    def direct1(self):
        self.s0[...] = lax.select_n(self.ocore == self.core, self.cb[...], self.half(self.core))
        self.b1[self.a] = self.s0[pl.ds(pl.multiple_of(self.a * 64, 64), 64), :]
        for t in (1, 2, 3):
            q = pl.multiple_of(lax.rem(self.a + t, 4) * 64, 64)
            self.send(self.s0.at[pl.ds(q, 64)], self.b1.at[self.a], shifted(self.me, self.ax[0], t))

    def direct3(self):
        self.s1[...] = pick(self.b1, self.oa)
        self.spread()

    def direct6(self):
        here = self.rows(self.a * 64, 64)
        for t in (1, 2, 3):
            self.send(here, here, shifted(self.me, self.ax[0], t))

    def step2(self):
        right = pl.multiple_of(lax.rem(self.a + 1, 4) * 64, 64)
        left = pl.multiple_of(lax.rem(self.a + 3, 4) * 64, 64)
        d = (self.oa - self.a) & 3
        ra = self.s0.at[pl.ds(right, 32)]
        ra[...] = lax.select_n(d == 3, ra[...], self.ra[...])
        lb = self.s0.at[pl.ds(pl.multiple_of(left + 32, 32), 32)]
        lb[...] = lax.select_n(d == 1, lb[...], self.rb[...])
        self.send(self.s0.at[pl.ds(right, 64)], self.rl, shifted(self.me, self.ax[0], 1))
        self.send(self.s0.at[pl.ds(left, 64)], self.rr, shifted(self.me, self.ax[0], 3))

    def step3(self):
        d = (self.oa - self.a) & 3
        mine = self.a * 64
        va = lax.select_n(d == 1, self.rl[0:32], self.rr[0:32])
        self.s1[0:32] = lax.select_n(d == 0, va, self.s0[pl.ds(pl.multiple_of(mine, 64), 32), :])
        vb = lax.select_n(d == 3, self.rr[32:64], self.rl[32:64])
        self.s1[32:64] = lax.select_n(d == 0, vb, self.s0[pl.ds(pl.multiple_of(mine + 32, 32), 32), :])
        self.spread()

    def spread(self):
        self.b2[self.b] = self.s1[pl.ds(pl.multiple_of(self.b * 16, 16), 16), :]
        for t in (1, 2, 3):
            q = lax.rem(self.b + t, 4) * 16
            self.send(self.s1.at[pl.ds(pl.multiple_of(q, 16), 16)], self.b2.at[self.b],
                      shifted(self.me, self.ax[1], t))

    def step4(self):
        self.b3[self.c] = pick(self.b2, self.ob)
        for t in (1, 2, 3):
            self.send(self.b3.at[self.c], self.b3.at[self.c], shifted(self.me, self.ax[2], t))

    def rows(self, start, count):
        return self.dst.at[self.r, pl.ds(pl.multiple_of(self.core * 256 + start, min(count, 64)), count), self.cols]

    def step5(self):
        here = self.rows(self.a * 64 + self.b * 16, 16)
        here[...] = pick(self.b3, self.oc)
        for t in (1, 2, 3):
            self.send(here, here, shifted(self.me, self.ax[1], t))

    def step6(self):
        here = self.rows(self.a * 64, 64)
        self.send(here, here, shifted(self.me, self.ax[0], 1))
        self.send(here, here, shifted(self.me, self.ax[0], 3))

    def step7(self):
        fa = self.rows(lax.rem(self.a + 3, 4) * 64, 32)
        fb = self.rows(lax.rem(self.a + 1, 4) * 64 + 32, 32)
        self.send(fa, fa, shifted(self.me, self.ax[0], 1))
        self.send(fb, fb, shifted(self.me, self.ax[0], 3))

    def step8(self):
        here = self.rows(0, 256)
        self.send(here, here, self.partner())

    def step9(self):
        pass


WHOLE = slice(None)
RING = [("step0", 1.7, 1.0, 256), ("step1", 0.7, 2.7, 64), ("step2", 1.4, 2.7, 128), ("step3", 1.0, 2.7, 48),
        ("step4", 1.0, 2.7, 48), ("step5", 1.0, 2.7, 48), ("step6", 1.4, 2.7, 128), ("step7", 0.7, 2.7, 64),
        ("step8", 1.7, 1.0, 256), ("step9", 0.0, 0.0, 0)]
DIRECT = [("step0", 1.7, 1.0, 256), ("direct1", 4.1, 3.0, 192), ("direct3", 1.0, 2.7, 48), ("step4", 1.0, 2.7, 48),
          ("step5", 1.0, 2.7, 48), ("direct6", 4.1, 3.0, 192), ("step8", 1.7, 1.0, 256), ("step9", 0.0, 0.0, 0)]
BATCHES = [
    (RING, 1, [("p", 0, slice(0, 128)), ("p", 0, slice(128, 256)), ("p", 0, slice(256, 512))]),
    (RING, 3, [("p", 1, WHOLE), ("p", 2, WHOLE), ("p", 3, WHOLE)]),
    (RING, 3, [("p", 4, WHOLE), ("p", 5, WHOLE), ("t", 0, WHOLE)]),
    (RING, 3, [("t", 1, WHOLE), ("t", 2, WHOLE), ("t", 3, WHOLE)]),
    (RING, 2, [("t", 4, WHOLE), ("t", 5, WHOLE)]),
]
ISSUE = {"step0": 0.1, "step1": 0.4, "direct1": 0.5}


def plan_order(units):
    order, done, now = [], set(), 0.0
    free = {"core": 0.0, "ici": 0.0}
    following = [0] * len(BATCHES)
    ready = [0.0] * len(BATCHES)
    left = dict(units)
    while True:
        steps = [(ready[b], b) for b, (form, _, _) in enumerate(BATCHES) if following[b] < len(form)]
        if not steps and not left:
            return order
        due = [b for t, b in steps if t <= now]
        if due:
            b = due[0]
            form, size, entries = BATCHES[b]
            s = following[b]
            name, wire, flight, _ = form[s]
            order.append(("step", b, s))
            now += ISSUE.get(name, 0.15) * size / 3
            if s == len(form) - 1:
                done.update(("block", k, r) for k, r, _ in entries)
            else:
                link = "core" if name in ("step0", "step8") else "ici"
                free[link] = max(now, free[link]) + wire * size / 3
                ready[b] = free[link] + flight
            following[b] += 1
            continue
        name = next((n for n, (_, needs) in left.items() if all(d in done for d in needs)), None)
        if name is not None:
            order.append(name)
            now += left.pop(name)[0]
            done.add(name)
            continue
        now = min(t for t, _ in steps)


def work_units():
    units = {}
    for q in range(4):
        units[("xnorm", q)] = (0.3, [])
    for r in range(ROUNDS):
        units[("minv", r)] = (0.5, [])
    for r in range(ROUNDS):
        units[("solve", r)] = (0.8 + 0.15 * r, [("block", "t", r), ("minv", r)]
                               + [("pair", r, s) for s in range(r)] + ([("solve", r - 1)] if r else []))
        units[("upd", r)] = (0.9, [("solve", r), ("block", "t", ROUNDS - 1)] + [("own", r, q) for q in range(4)]
                             + ([("upd", r - 1)] if r else []))
    for r in range(ROUNDS):
        units[("bnorm", r)] = (0.3, [("block", "p", r)])
        for s in range(r):
            units[("pair", r, s)] = (0.3, [("bnorm", r), ("bnorm", s)])
        for q in range(4):
            units[("own", r, q)] = (0.3, [("bnorm", r), ("xnorm", q)])
    return units


ORDER = plan_order(work_units())


def buffers(width, dtype):
    shapes = [(256,), (256,), (256,), (4, 64), (64,), (4, 16), (4, 16)]
    return [pltpu.VMEM((ROUNDS,) + s + (width,), dtype) for s in shapes]


def to_row(col):
    return jnp.transpose(jnp.broadcast_to(col, (col.shape[0], 128)))[0:1, :]


def norm(block):
    sq = jnp.square(block.astype(jnp.float32))
    return (GAMMA * LOG2E) * jnp.sum(sq, axis=1, keepdims=True)


def kmat(x, xcol, b, brow):
    inner = lax.dot_general(x, b, NT, preferred_element_type=jnp.float32)
    return jnp.exp2((2.0 * GAMMA * LOG2E) * inner - (xcol + brow)).astype(jnp.bfloat16)


def mm(a, b):
    return lax.dot_general(a, b, NN, preferred_element_type=jnp.float32)


def split(v):
    hi = v.astype(jnp.bfloat16)
    return hi, (v - hi.astype(jnp.float32)).astype(jnp.bfloat16)


def whole_kernel(total, plan_ref, pts_hbm, tgt_hbm, inv_hbm, res_hbm, steps_hbm, out, *scratch):
    bufp, buft = scratch[:7], scratch[7:14]
    (ss, rs, pts, res, bp, bt, minv, mh, ml, kown, kp1, kp2, kp3, kp4, kp5, xcol, bcol, brow, steps, sh, part,
     mine_loss, g1, mid, g2, lsem, local, msem, osem) = scratch[14:]
    kp = [None, kp1, kp2, kp3, kp4, kp5]
    me = coords()
    x, y, z, core = me
    first = (lax.axis_index("row") * 16 + lax.axis_index("col")) * 4
    loads = [pltpu.make_async_copy(pts_hbm, pts, local.at[0]), pltpu.make_async_copy(tgt_hbm, res, local.at[1])]
    for c in loads:
        c.start()
    fetch = [pltpu.make_async_copy(inv_hbm.at[r], minv.at[r % 2], msem.at[r]) for r in range(ROUNDS)]
    fetch[0].start()
    fetch[1].start()
    near, far, near_id, far_id = [], [], x * 2 + core, y * 4 + z
    for t in range(1, 8):
        v = lax.rem(near_id + t, 8)
        near.append(device(lax.div(v, 2), y, z, lax.rem(v, 2)))
    for t in range(1, 16):
        v = lax.rem(far_id + t, 16)
        far.append(device(x, lax.div(v, 4), lax.rem(v, 4), core))
    peers = [device(x, y, z, 1 - core)] + [shifted(me, ax, t) for ax in range(3) for t in (1, 2, 3)]
    barrier = pltpu.get_barrier_semaphore()
    for dev in peers:
        pl.semaphore_signal(barrier, inc=1, device_id=dev, device_id_type=MESH)
    for c in loads:
        c.wait()

    batches = []
    for b, (_, _, entries) in enumerate(BATCHES):
        made = []
        for color, (kind, r, cols) in enumerate(entries):
            src, dst, bufs = (pts, bp, bufp) if kind == "p" else (res, bt, buft)
            made.append(Chunk(color, r, cols, me, plan_ref, src, dst, bufs, (ss.at[b], rs.at[b])))
            made[-1].stage_half()
        batches.append(made)
    pl.semaphore_wait(barrier, len(peers))

    def await_ref(ref, sem):
        pltpu.make_async_copy(ref, ref, sem).wait()

    def await_bytes(kib, sem):
        await_ref(kown.at[0:kib], sem)

    def comm_step(b, s):
        form, size, _ = BATCHES[b]
        if s:
            await_bytes(form[s - 1][3] * size, rs.at[b, s - 1])
        for ch in batches[b]:
            ch.stage = s
            getattr(ch, form[s][0])()

    writes = []

    def do_minv(r):
        fetch[r].wait()
        mh[r], ml[r] = split(minv[r % 2])
        if r + 2 < ROUNDS:
            fetch[r + 2].start()

    def do_bnorm(r):
        c = norm(bp[r])
        bcol[r] = c
        brow[r] = to_row(c)

    def do_xnorm(q):
        xcol[q] = norm(pts[q])

    def do_pair(r, s):
        kp[r][:, s * BLK:(s + 1) * BLK] = kmat(bp[r], bcol[r], bp[s], brow[s])

    def own_rows(r, q):
        start = (r * 4 + q) * BLK
        return slice(start, start + BLK)

    def do_own(r, q):
        kown[own_rows(r, q), :] = kmat(pts[q], xcol[q], bp[r], brow[r])

    def do_solve(r):
        v = bt[r]
        for s in range(r):
            v = v - jnp.where(plan_ref[s] == plan_ref[r], RIDGE, 0.0) * steps[s]
        if r:
            v = v - mm(kp[r][...], sh[0:r * BLK, :])
        yh, yl = split(v)
        step = mm(mh[r], yh) + (mm(mh[r], yl) + mm(ml[r], yh))
        steps[r] = step
        sh[r * BLK:(r + 1) * BLK, :] = step.astype(jnp.bfloat16)

    def do_upd(r):
        acc = jnp.zeros((8, K), jnp.float32)
        for q in range(4):
            mine = jnp.where(plan_ref[r] == first + q, RIDGE, 0.0)
            new = res[q] - mm(kown[own_rows(r, q), :], sh[r * BLK:(r + 1) * BLK, :]) - mine * steps[r]
            res[q] = new
            acc = acc + jnp.sum((new * new).reshape(64, 8, K), axis=0)
        part[r:r + 1, :] = jnp.sum(acc[:, :128] + acc[:, 128:], axis=0, keepdims=True)
        c = pltpu.make_async_copy(sh.at[r * BLK:(r + 1) * BLK, :], steps_hbm.at[r], osem.at[r])
        c.start()
        writes.append(c)

    part[...] = jnp.zeros_like(part)
    todo = {"minv": do_minv, "bnorm": do_bnorm, "xnorm": do_xnorm, "pair": do_pair, "own": do_own,
            "solve": do_solve, "upd": do_upd}
    for item in ORDER:
        if item[0] == "step":
            comm_step(*item[1:])
        else:
            todo[item[0]](*item[1:])

    mine_loss[...] = part[...]
    g1[near_id] = part[...]
    for dev in near:
        pltpu.make_async_remote_copy(mine_loss, g1.at[near_id], lsem.at[0], lsem.at[1], device_id=dev,
                                     device_id_type=MESH).start()
    c = pltpu.make_async_copy(res, res_hbm, osem.at[ROUNDS])
    c.start()
    writes.append(c)
    await_ref(g1.at[0:7], lsem.at[1])
    mid[...] = jnp.sum(g1[...], axis=0)
    g2[far_id] = mid[...]
    for dev in far:
        pltpu.make_async_remote_copy(mid, g2.at[far_id], lsem.at[2], lsem.at[3], device_id=dev,
                                     device_id_type=MESH).start()
    for b, (form, size, _) in enumerate(BATCHES):
        await_bytes(sum(f[3] for f in form) * size, ss.at[b])
    await_ref(g1.at[0:7], lsem.at[0])
    await_ref(g2.at[0:15], lsem.at[3])
    whole = jnp.sum(g2[...], axis=0)
    for r in range(ROUNDS):
        out[r] = jnp.sum(whole[r:r + 1, :]) * (1.0 / total)
    await_ref(g2.at[0:15], lsem.at[2])
    for c in writes:
        c.wait()


def on_device(points, targets, plan, block_inverse):
    rows = points.shape[0]
    total = float(rows * 128 * targets.shape[1])
    anywhere = pl.BlockSpec(memory_space=pl.ANY)
    smem = pl.BlockSpec(memory_space=pltpu.SMEM)
    f32, b16, dma = jnp.float32, jnp.bfloat16, pltpu.SemaphoreType.DMA
    res, steps, losses = pl.pallas_call(
        lambda *refs: whole_kernel(total, *refs),
        out_shape=(jax.ShapeDtypeStruct((4, BLK, K), f32), jax.ShapeDtypeStruct((ROUNDS, BLK, K), b16),
                   jax.ShapeDtypeStruct((ROUNDS,), f32)),
        in_specs=[smem, anywhere, anywhere, anywhere],
        out_specs=(anywhere, anywhere, smem),
        scratch_shapes=buffers(F, b16) + buffers(K, f32) + [
            dma((len(BATCHES),)), dma((len(BATCHES), 9)),
            pltpu.VMEM((4, BLK, F), b16), pltpu.VMEM((4, BLK, K), f32),
            pltpu.VMEM((ROUNDS, BLK, F), b16), pltpu.VMEM((ROUNDS, BLK, K), f32),
            pltpu.VMEM((2, BLK, BLK), f32), pltpu.VMEM((ROUNDS, BLK, BLK), b16), pltpu.VMEM((ROUNDS, BLK, BLK), b16),
            pltpu.VMEM((ROUNDS * 4 * BLK, BLK), b16),
            *[pltpu.VMEM((BLK, r * BLK), b16) for r in range(1, ROUNDS)],
            pltpu.VMEM((4, BLK, 1), f32), pltpu.VMEM((ROUNDS, BLK, 1), f32), pltpu.VMEM((ROUNDS, 1, BLK), f32),
            pltpu.VMEM((ROUNDS, BLK, K), f32), pltpu.VMEM((ROUNDS * BLK, K), b16), pltpu.VMEM((8, 128), f32),
            pltpu.VMEM((8, 128), f32), pltpu.VMEM((8, 8, 128), f32), pltpu.VMEM((8, 128), f32),
            pltpu.VMEM((16, 8, 128), f32),
            dma((4,)), dma((2,)), dma((ROUNDS,)), dma((ROUNDS + 1,)),
        ],
        compiler_params=pltpu.CompilerParams(collective_id=0, has_side_effects=True, vmem_limit_bytes=67043328),
        name="block_ridge",
    )(plan, points.reshape(4, BLK, F), targets.reshape(4, BLK, K), block_inverse)
    return res.reshape(rows, K), steps, losses


def solution(mesh):
    placed = (P(("row", "col"), None), P(("row", "col"), None), P(), P())
    return jax.shard_map(
        on_device,
        mesh=mesh,
        in_specs=placed,
        out_specs=(P(("row", "col"), None), P(), P()),
        check_vma=False,
    )
```

time: 95 us -> 83.7 us (0.88)
  Pallas kernels: 89.4 us -> 78 us
    pallas_call x1, Pallas kernels: 89.4 us -> 78 us  [on_device(): pl.pallas_call(lambda *refs: whole_kernel(total, *refs), out_shape=(jax.S...]
where the time goes in v3:
time: 83.7 us; the launch traced here: 83.5 us
  Pallas kernels  78 us (93%)
  local copies, waits for them, and re-layouts  4.82 us (6%)
    pallas_call x1, Pallas kernels, on_device(): pl.pallas_call(lambda *refs: whole_kernel(total, *refs), out_shape=(jax.S...  78 us
    unnamed x7, local copies, waits for them, and re-layouts  4.82 us

profile of v3, /device:TPU:1, one launch (start us, length us, event | category | flops | bytes accessed | tf_op | source)
XLA Modules:
  0.0 83.5 jit_solution(12852753505817096923)
XLA Ops:
  0.6 78.0 %block_ridge.1 = (f32[4,512,256]{2,1,0:T(8,128)}, bf16[6,512,256]{2,1,0:T(8,128)(2,1)}, f32[6]{0:T(128)}) custom-call(s32[6]{0:T(128)} %refs_0_.1, bf16[4,512,512]{2,1,0:T(8,128)(2,1)} %bitcast.4, f32[4,512,256]{2,1,0:T(8,128)} %bitcast.5, f32[6,512,512]{2,1,0:T(8,128)} %refs_3_.1), custom_call_target="tpu_custom_call" | custom-call | tf_op jit(solution)/shard_map/block_ridge/pallas_call | solution.py:410
  78.7 0.0 copy-start
  78.7 3.2 %copy.10 = f32[2048,256]{1,0:T(8,128)} copy(f32[2048,256]{1,0:T(8,128)} %bitcast.3) | data formatting | bytes 4194304
  81.8 0.0 copy-done
  81.8 0.0 copy-start.1
  81.9 1.1 %copy.11 = bf16[6,512,256]{2,1,0:T(8,128)(2,1)} copy(bf16[6,512,256]{2,1,0:T(8,128)(2,1)S(1)} %copy-done) | data formatting | bytes 3145728
  83.0 0.0 copy-done.1
  83.0 0.5 copy.12
Async XLA Ops:
  78.7 3.2 %copy-start = (bf16[6,512,256]{2,1,0:T(8,128)(2,1)S(1)}, bf16[6,512,256]{2,1,0:T(8,128)(2,1)}, u32[]{:S(2)}) copy-start(bf16[6,512,256]{2,1,0:T(8,128)(2,1)} %get-tuple-element.13) | copy-start | bytes 4718596
  81.8 1.1 %copy-start.1 = (f32[6]{0:T(128)S(1)}, f32[6]{0:T(128)}, u32[]{:S(2)}) copy-start(f32[6]{0:T(128)} %get-tuple-element.14) | copy-start | bytes 76

commit v4 on v3

--- a/solution.py
+++ b/solution.py
@@ -170,11 +170,10 @@
 DIRECT = [("step0", 1.7, 1.0, 256), ("direct1", 4.1, 3.0, 192), ("direct3", 1.0, 2.7, 48), ("step4", 1.0, 2.7, 48),
           ("step5", 1.0, 2.7, 48), ("direct6", 4.1, 3.0, 192), ("step8", 1.7, 1.0, 256), ("step9", 0.0, 0.0, 0)]
 BATCHES = [
-    (RING, 1, [("p", 0, slice(0, 128)), ("p", 0, slice(128, 256)), ("p", 0, slice(256, 512))]),
-    (RING, 3, [("p", 1, WHOLE), ("p", 2, WHOLE), ("p", 3, WHOLE)]),
-    (RING, 3, [("p", 4, WHOLE), ("p", 5, WHOLE), ("t", 0, WHOLE)]),
-    (RING, 3, [("t", 1, WHOLE), ("t", 2, WHOLE), ("t", 3, WHOLE)]),
-    (RING, 2, [("t", 4, WHOLE), ("t", 5, WHOLE)]),
+    (DIRECT, 3, [("p", 0, WHOLE), ("p", 1, WHOLE), ("p", 2, WHOLE)]),
+    (DIRECT, 3, [("p", 3, WHOLE), ("p", 4, WHOLE), ("p", 5, WHOLE)]),
+    (RING, 3, [("t", 0, WHOLE), ("t", 1, WHOLE), ("t", 2, WHOLE)]),
+    (RING, 3, [("t", 3, WHOLE), ("t", 4, WHOLE), ("t", 5, WHOLE)]),
 ]
 ISSUE = {"step0": 0.1, "step1": 0.4, "direct1": 0.5}
 
@@ -197,6 +196,8 @@
             name, wire, flight, _ = form[s]
             order.append(("step", b, s))
             now += ISSUE.get(name, 0.15) * size / 3
+            if s == 1:
+                done.update(("taken", k, r) for k, r, _ in entries)
             if s == len(form) - 1:
                 done.update(("block", k, r) for k, r, _ in entries)
             else:
@@ -214,6 +215,22 @@
         now = min(t for t, _ in steps)
 
 
+def grouped(order, units, most):
+    out, size = [], 0.0
+    for item in order:
+        if item[0] == "step":
+            out.append(item)
+            continue
+        us = units[item][0]
+        if out and out[-1][0] == "group" and size + us <= most and out[-1][1][-1][0] != "solve":
+            out[-1][1].append(item)
+            size += us
+        else:
+            out.append(("group", [item]))
+            size = us
+    return out
+
+
 def work_units():
     units = {}
     for q in range(4):
@@ -223,18 +240,19 @@
     for r in range(ROUNDS):
         units[("solve", r)] = (0.8 + 0.15 * r, [("block", "t", r), ("minv", r)]
                                + [("pair", r, s) for s in range(r)] + ([("solve", r - 1)] if r else []))
-        units[("upd", r)] = (0.9, [("solve", r), ("block", "t", ROUNDS - 1)] + [("own", r, q) for q in range(4)]
+        units[("upd", r)] = (0.9, [("solve", r)] + [("own", r, h) for h in range(2)]
+                             + [("taken", "t", t) for t in range(ROUNDS)]
                              + ([("upd", r - 1)] if r else []))
     for r in range(ROUNDS):
         units[("bnorm", r)] = (0.3, [("block", "p", r)])
         for s in range(r):
             units[("pair", r, s)] = (0.3, [("bnorm", r), ("bnorm", s)])
-        for q in range(4):
-            units[("own", r, q)] = (0.3, [("bnorm", r), ("xnorm", q)])
+        for h in range(2):
+            units[("own", r, h)] = (0.6, [("bnorm", r), ("xnorm", 3)])
     return units
 
 
-ORDER = plan_order(work_units())
+ORDER = grouped(plan_order(work_units()), work_units(), 2.6)
 
 
 def buffers(width, dtype):
@@ -267,7 +285,7 @@
 
 def whole_kernel(total, plan_ref, pts_hbm, tgt_hbm, inv_hbm, res_hbm, steps_hbm, out, *scratch):
     bufp, buft = scratch[:7], scratch[7:14]
-    (ss, rs, pts, res, bp, bt, minv, mh, ml, kown, kp1, kp2, kp3, kp4, kp5, xcol, bcol, brow, steps, sh, part,
+    (ss, rs, pts, res, bp, bt, minv, mhl, kown, kp1, kp2, kp3, kp4, kp5, xcol, bcol, brow, steps, sh, part,
      mine_loss, g1, mid, g2, lsem, local, msem, osem) = scratch[14:]
     kp = [None, kp1, kp2, kp3, kp4, kp5]
     me = coords()
@@ -317,11 +335,14 @@
             ch.stage = s
             getattr(ch, form[s][0])()
 
-    writes = []
+
+    def write(r):
+        return pltpu.make_async_copy(sh.at[r * BLK:(r + 1) * BLK, :], steps_hbm.at[r], osem.at[r])
+
 
     def do_minv(r):
         fetch[r].wait()
-        mh[r], ml[r] = split(minv[r % 2])
+        mhl[r, 0:BLK], mhl[r, BLK:2 * BLK] = split(minv[r % 2])
         if r + 2 < ROUNDS:
             fetch[r + 2].start()
 
@@ -336,12 +357,11 @@
     def do_pair(r, s):
         kp[r][:, s * BLK:(s + 1) * BLK] = kmat(bp[r], bcol[r], bp[s], brow[s])
 
-    def own_rows(r, q):
-        start = (r * 4 + q) * BLK
-        return slice(start, start + BLK)
-
-    def do_own(r, q):
-        kown[own_rows(r, q), :] = kmat(pts[q], xcol[q], bp[r], brow[r])
+    def do_own(r, h):
+        start = (r * 4 + 2 * h) * BLK
+        x2 = pts[2 * h:2 * h + 2].reshape(2 * BLK, F)
+        c2 = xcol[2 * h:2 * h + 2].reshape(2 * BLK, 1)
+        kown[start:start + 2 * BLK, :] = kmat(x2, c2, bp[r], brow[r])
 
     def do_solve(r):
         v = bt[r]
@@ -350,21 +370,21 @@
         if r:
             v = v - mm(kp[r][...], sh[0:r * BLK, :])
         yh, yl = split(v)
-        step = mm(mh[r], yh) + (mm(mh[r], yl) + mm(ml[r], yh))
+        both = mm(mhl[r], yh)
+        step = both[0:BLK] + (mm(mhl[r, 0:BLK], yl) + both[BLK:2 * BLK])
         steps[r] = step
         sh[r * BLK:(r + 1) * BLK, :] = step.astype(jnp.bfloat16)
 
     def do_upd(r):
         acc = jnp.zeros((8, K), jnp.float32)
+        prod = mm(kown[r * 4 * BLK:(r + 1) * 4 * BLK, :], sh[r * BLK:(r + 1) * BLK, :])
         for q in range(4):
             mine = jnp.where(plan_ref[r] == first + q, RIDGE, 0.0)
-            new = res[q] - mm(kown[own_rows(r, q), :], sh[r * BLK:(r + 1) * BLK, :]) - mine * steps[r]
+            new = res[q] - prod[q * BLK:(q + 1) * BLK] - mine * steps[r]
             res[q] = new
             acc = acc + jnp.sum((new * new).reshape(64, 8, K), axis=0)
         part[r:r + 1, :] = jnp.sum(acc[:, :128] + acc[:, 128:], axis=0, keepdims=True)
-        c = pltpu.make_async_copy(sh.at[r * BLK:(r + 1) * BLK, :], steps_hbm.at[r], osem.at[r])
-        c.start()
-        writes.append(c)
+        write(r).start()
 
     part[...] = jnp.zeros_like(part)
     todo = {"minv": do_minv, "bnorm": do_bnorm, "xnorm": do_xnorm, "pair": do_pair, "own": do_own,
@@ -373,16 +393,19 @@
         if item[0] == "step":
             comm_step(*item[1:])
         else:
-            todo[item[0]](*item[1:])
+
+            @pl.when(core >= 0)
+            def _():
+                for name in item[1]:
+                    todo[name[0]](*name[1:])
 
     mine_loss[...] = part[...]
     g1[near_id] = part[...]
     for dev in near:
         pltpu.make_async_remote_copy(mine_loss, g1.at[near_id], lsem.at[0], lsem.at[1], device_id=dev,
                                      device_id_type=MESH).start()
-    c = pltpu.make_async_copy(res, res_hbm, osem.at[ROUNDS])
-    c.start()
-    writes.append(c)
+    put = pltpu.make_async_copy(res, res_hbm, osem.at[ROUNDS])
+    put.start()
     await_ref(g1.at[0:7], lsem.at[1])
     mid[...] = jnp.sum(g1[...], axis=0)
     g2[far_id] = mid[...]
@@ -397,8 +420,9 @@
     for r in range(ROUNDS):
         out[r] = jnp.sum(whole[r:r + 1, :]) * (1.0 / total)
     await_ref(g2.at[0:15], lsem.at[2])
-    for c in writes:
-        c.wait()
+    put.wait()
+    for r in range(ROUNDS):
+        write(r).wait()
 
 
 def on_device(points, targets, plan, block_inverse):
@@ -417,7 +441,7 @@
             dma((len(BATCHES),)), dma((len(BATCHES), 9)),
             pltpu.VMEM((4, BLK, F), b16), pltpu.VMEM((4, BLK, K), f32),
             pltpu.VMEM((ROUNDS, BLK, F), b16), pltpu.VMEM((ROUNDS, BLK, K), f32),
-            pltpu.VMEM((2, BLK, BLK), f32), pltpu.VMEM((ROUNDS, BLK, BLK), b16), pltpu.VMEM((ROUNDS, BLK, BLK), b16),
+            pltpu.VMEM((2, BLK, BLK), f32), pltpu.VMEM((ROUNDS, 2 * BLK, BLK), b16),
             pltpu.VMEM((ROUNDS * 4 * BLK, BLK), b16),
             *[pltpu.VMEM((BLK, r * BLK), b16) for r in range(1, ROUNDS)],
             pltpu.VMEM((4, BLK, 1), f32), pltpu.VMEM((ROUNDS, BLK, 1), f32), pltpu.VMEM((ROUNDS, 1, BLK), f32),

time: 83.7 us -> 80 us (0.956)
  Pallas kernels: 78 us -> 74.3 us
    pallas_call x1, Pallas kernels: 78 us -> 74.3 us  [on_device(): pl.pallas_call(lambda *refs: whole_kernel(total, *refs), out_shape=(jax.S...]
where the time goes in v4:
time: 80 us; the launch traced here: 79.8 us
  Pallas kernels  74.3 us (93%)
  local copies, waits for them, and re-layouts  4.82 us (6%)
    pallas_call x1, Pallas kernels, on_device(): pl.pallas_call(lambda *refs: whole_kernel(total, *refs), out_shape=(jax.S...  74.3 us
    unnamed x7, local copies, waits for them, and re-layouts  4.82 us

profile of v4, /device:TPU:1, one launch (start us, length us, event | category | flops | bytes accessed | tf_op | source)
XLA Modules:
  0.0 79.8 jit_solution(17381470900606857619)
XLA Ops:
  0.6 74.3 %block_ridge.1 = (f32[4,512,256]{2,1,0:T(8,128)}, bf16[6,512,256]{2,1,0:T(8,128)(2,1)}, f32[6]{0:T(128)}) custom-call(s32[6]{0:T(128)} %refs_0_.1, bf16[4,512,512]{2,1,0:T(8,128)(2,1)} %bitcast.4, f32[4,512,256]{2,1,0:T(8,128)} %bitcast.5, f32[6,512,512]{2,1,0:T(8,128)} %refs_3_.1), custom_call_target="tpu_custom_call" | custom-call | tf_op jit(solution)/shard_map/block_ridge/pallas_call | solution.py:434
  75.0 0.0 copy-start
  75.0 3.2 %copy.10 = f32[2048,256]{1,0:T(8,128)} copy(f32[2048,256]{1,0:T(8,128)} %bitcast.3) | data formatting | bytes 4194304
  78.2 0.0 copy-done
  78.2 0.0 copy-start.1
  78.2 1.1 %copy.11 = bf16[6,512,256]{2,1,0:T(8,128)(2,1)} copy(bf16[6,512,256]{2,1,0:T(8,128)(2,1)S(1)} %copy-done) | data formatting | bytes 3145728
  79.3 0.0 copy-done.1
  79.3 0.5 copy.12
Async XLA Ops:
  75.0 3.2 %copy-start = (bf16[6,512,256]{2,1,0:T(8,128)(2,1)S(1)}, bf16[6,512,256]{2,1,0:T(8,128)(2,1)}, u32[]{:S(2)}) copy-start(bf16[6,512,256]{2,1,0:T(8,128)(2,1)} %get-tuple-element.13) | copy-start | bytes 4718596
  78.2 1.1 %copy-start.1 = (f32[6]{0:T(128)S(1)}, f32[6]{0:T(128)}, u32[]{:S(2)}) copy-start(f32[6]{0:T(128)} %get-tuple-element.14) | copy-start | bytes 76

commit v5 on v4

--- a/solution.py
+++ b/solution.py
@@ -425,6 +425,26 @@
         write(r).wait()
 
 
+def put_kernel(res, steps, losses, res_out, steps_out, losses_out, res_vmem, steps_vmem, sem):
+    moves = []
+    for q in range(4):
+        moves.append((pltpu.make_async_copy(res.at[q], res_vmem.at[q], sem.at[q]),
+                      pltpu.make_async_copy(res_vmem.at[q], res_out.at[q], sem.at[q])))
+    for q in range(3):
+        two = pl.ds(2 * q, 2)
+        moves.append((pltpu.make_async_copy(steps.at[two], steps_vmem.at[two], sem.at[4 + q]),
+                      pltpu.make_async_copy(steps_vmem.at[two], steps_out.at[two], sem.at[4 + q])))
+    for take, _ in moves:
+        take.start()
+    for r in range(ROUNDS):
+        losses_out[r] = losses[r]
+    for take, give in moves:
+        take.wait()
+        give.start()
+    for _, give in moves:
+        give.wait()
+
+
 def on_device(points, targets, plan, block_inverse):
     rows = points.shape[0]
     total = float(rows * 128 * targets.shape[1])
@@ -453,6 +473,15 @@
         compiler_params=pltpu.CompilerParams(collective_id=0, has_side_effects=True, vmem_limit_bytes=67043328),
         name="block_ridge",
     )(plan, points.reshape(4, BLK, F), targets.reshape(4, BLK, K), block_inverse)
+    res, steps, losses = pl.pallas_call(
+        put_kernel,
+        out_shape=(jax.ShapeDtypeStruct((4, BLK, K), f32), jax.ShapeDtypeStruct((ROUNDS, BLK, K), b16),
+                   jax.ShapeDtypeStruct((ROUNDS,), f32)),
+        in_specs=[anywhere, anywhere, smem],
+        out_specs=(anywhere, anywhere, smem),
+        scratch_shapes=[pltpu.VMEM((4, BLK, K), f32), pltpu.VMEM((ROUNDS, BLK, K), b16), dma((7,))],
+        name="put_results",
+    )(res, steps, losses)
     return res.reshape(rows, K), steps, losses
 
 

time: 80 us -> 79.5 us (level)
  local copies, waits for them, and re-layouts: 4.82 us -> 0 us
  Pallas kernels: 74.3 us -> 78.5 us
    unnamed x7 -> x0, local copies, waits for them, and re-layouts: 4.82 us -> none
    pallas_call x0 -> x1, Pallas kernels: none -> 4.14 us  [on_device(): pl.pallas_call(put_kernel, out_shape=(jax.ShapeDtypeStruct((4, BLK, K), f...]
where the time goes in v5:
time: 79.5 us; the launch traced here: 79.3 us
  Pallas kernels  78.5 us (99%)
  between operations  0.8 us (1%)
    pallas_call x1, Pallas kernels, on_device(): pl.pallas_call(lambda *refs: whole_kernel(total, *refs), out_shape=(jax.S...  74.3 us
    pallas_call x1, Pallas kernels, on_device(): pl.pallas_call(put_kernel, out_shape=(jax.ShapeDtypeStruct((4, BLK, K), f...  4.14 us

profile of v5, /device:TPU:1, one launch (start us, length us, event | category | flops | bytes accessed | tf_op | source)
XLA Modules:
  0.0 79.3 jit_solution(211514567566717459)
XLA Ops:
  0.6 74.3 %block_ridge.1 = (f32[4,512,256]{2,1,0:T(8,128)}, bf16[6,512,256]{2,1,0:T(8,128)(2,1)}, f32[6]{0:T(128)}) custom-call(s32[6]{0:T(128)} %refs_0_.1, bf16[4,512,512]{2,1,0:T(8,128)(2,1)} %bitcast.3, f32[4,512,256]{2,1,0:T(8,128)} %bitcast.4, f32[6,512,512]{2,1,0:T(8,128)} %refs_3_.1), custom_call_target="tpu_custom_call" | custom-call | tf_op jit(solution)/shard_map/block_ridge/pallas_call | solution.py:454
  75.0 4.1 %put_results.1 = (f32[4,512,256]{2,1,0:T(8,128)}, bf16[6,512,256]{2,1,0:T(8,128)(2,1)}, f32[6]{0:T(128)}) custom-call(f32[4,512,256]{2,1,0:T(8,128)} %get-tuple-element.9.res, bf16[6,512,256]{2,1,0:T(8,128)(2,1)} %get-tuple-element.10.steps, f32[6]{0:T(128)} %get-tuple-element.11.losses), custom_call_target="tpu_custom_call" | custom-call | tf_op jit(solution)/shard_map/put_results/pallas_call | solution.py:476
